TPU v7x, 256 devices: a whole 4x4x8 slice. The times are simulated.
256 devices in a mesh: dp: 8 (over x, core), group: 32 (over z, y).
Axes of the slice: x: 4, y: 4, z: 8, core: 2. Of those that a mesh axis runs over, the one named last changes fastest.
Arguments:
- embeds: bfloat16 [65536, 1024], P(('dp', 'group')), may hold values from -6 to 6
- row_ids: int32 [65536], P(('dp', 'group')), may hold values from 0 to 63
- neighbors: int32 [256, 3], P('dp'), may hold values from 0 to 31, as said below
- w_first: bfloat16 [1024, 4096], P(None, 'dp'), may hold values from -0.1875 to 0.1875
- w_second: bfloat16 [4096, 1024], P('dp'), may hold values from -0.09375 to 0.09375
Outputs:
- grad_first: float32 [1024, 4096], P('group', 'dp')
- grad_second: float32 [4096, 1024], P('dp', 'group')
- grad_unit: float32 [65536, 1024], P(('dp', 'group'))
Inputs may be any that keep to these rules, and one draw needn't show every extreme that they name: `neighbors`: within a row the 3 entries differ from one another and from the row's own index b % 32.
All inputs are finite; a program needn't handle non-finite values.
Results may differ from a plain program's by a relative error of at most 0.013.
Values may be sent and summed in bfloat16 or wider, within the bound.
No kernel may reach another device: no remote copies, remote signals or barrier semaphores. Data moves between devices by JAX's collectives and lax.ppermute only.
A program may use at most 64 MiB of HBM per device.

v0:
```python
import jax
import jax.numpy as jnp
from jax import lax
from jax.sharding import PartitionSpec as P

EPS = 1e-06
TEMP = 10.0
SHIFT = -5.0


def gelu_fwd(value):
    return jax.nn.gelu(value, approximate=True)


def gelu_back(pre, grad):
    _, back = jax.vjp(gelu_fwd, pre)
    return back(grad)[0]


def per_device(embeds, row_ids, neighbors, w_first, w_second):
    owners = lax.axis_size("group")
    block = embeds.shape[0]
    piece = block // owners
    width = w_second.shape[1]
    listed = neighbors.shape[1]
    gathered = lax.all_gather(embeds, "dp", axis=0, tiled=True)
    pre = jnp.dot(gathered, w_first, preferred_element_type=jnp.float32)
    hidden = gelu_fwd(pre).astype(jnp.bfloat16)
    proj = lax.psum_scatter(
        jnp.dot(hidden, w_second, preferred_element_type=jnp.float32).astype(jnp.bfloat16),
        "dp",
        scatter_dimension=0,
        tiled=True,
    ).astype(jnp.float32)
    inv = lax.rsqrt(jnp.mean(proj * proj, axis=-1, keepdims=True) + EPS)
    unit = proj * inv
    unit_b = unit.astype(jnp.bfloat16)
    held, held_ids = (
        lax.all_to_all(
            unit_b.reshape(owners, piece, width), "group", split_axis=0, concat_axis=0, tiled=True
        ),
        lax.all_to_all(
            row_ids.reshape(owners, piece), "group", split_axis=0, concat_axis=0, tiled=True
        ),
    )
    order = neighbors.T
    outgoing = jnp.take(held, order, axis=0)
    outgoing_ids = jnp.take(held_ids, order, axis=0)
    fetched, fetched_ids = (
        lax.all_to_all(outgoing, "group", split_axis=1, concat_axis=1, tiled=True),
        lax.all_to_all(outgoing_ids, "group", split_axis=1, concat_axis=1, tiled=True),
    )
    cand = jnp.concatenate([unit_b[None], fetched.reshape(listed, block, width)], 0)
    cand_ids = jnp.concatenate([row_ids[None], fetched_ids.reshape(listed, block)], 0)
    logits = (
        TEMP / width * jnp.einsum("rp,kcp->krc", unit_b, cand, preferred_element_type=jnp.float32)
        + SHIFT
    )
    sign = jnp.where(row_ids[None, :, None] == cand_ids[:, None, :], 1.0, -1.0).astype(jnp.float32)
    weight = (-sign * jax.nn.sigmoid(-sign * logits) * (TEMP / width)).astype(jnp.bfloat16)
    grad_own = jnp.einsum("krc,kcp->rp", weight, cand, preferred_element_type=jnp.float32)
    grad_cand = jnp.einsum("krc,rp->kcp", weight, unit_b, preferred_element_type=jnp.float32)
    returned = lax.all_to_all(
        grad_cand[1:].reshape(listed, owners, piece, width),
        "group",
        split_axis=1,
        concat_axis=1,
        tiled=True,
    )
    select = (order[:, :, None] == jnp.arange(owners, dtype=jnp.int32)[None, None, :]).astype(
        jnp.float32
    )
    summed = jnp.einsum("krb,krqp->bqp", select, returned, precision=lax.Precision.HIGHEST)
    collected = lax.all_to_all(summed, "group", split_axis=0, concat_axis=0, tiled=True)
    grad_unit = grad_own + grad_cand[0] + collected.reshape(block, width)
    grad_proj = inv * (grad_unit - unit * jnp.mean(unit * grad_unit, axis=-1, keepdims=True))
    grad_all = lax.all_gather(grad_proj.astype(jnp.bfloat16), "dp", axis=0, tiled=True)
    second_local = lax.dot_general(
        hidden, grad_all, (((0,), (0,)), ((), ())), preferred_element_type=jnp.float32
    )
    grad_hidden = lax.dot_general(
        grad_all, w_second, (((1,), (1,)), ((), ())), preferred_element_type=jnp.float32
    )
    grad_pre = gelu_back(pre, grad_hidden).astype(jnp.bfloat16)
    first_local = lax.dot_general(
        gathered, grad_pre, (((0,), (0,)), ((), ())), preferred_element_type=jnp.float32
    )
    first_out, second_out = (
        lax.psum_scatter(first_local, "group", scatter_dimension=0, tiled=True),
        lax.psum_scatter(second_local, "group", scatter_dimension=1, tiled=True),
    )
    return (first_out, second_out, grad_unit)


def solution(mesh):
    in_specs = (
        P(("dp", "group"), None),
        P(("dp", "group")),
        P("dp", None),
        P(None, "dp"),
        P("dp", None),
    )
    out_specs = (P("group", "dp"), P("dp", "group"), P(("dp", "group"), None))
    return jax.shard_map(
        per_device, mesh=mesh, in_specs=in_specs, out_specs=out_specs, check_vma=False
    )
```

profile of v0, /device:TPU:4, one launch (start us, length us, event | category | flops | bytes accessed | tf_op | source)
XLA Modules:
  0.0 792.0 jit_solution(12244141082356973376)
XLA Ops:
  8.0 38.2 %all-gather.3.cloned.1.call-done = bf16[2048,1024]{1,0:T(8,128)(2,1)} async-done(((bf16[256,1024]{1,0:T(8,128)(2,1)}), bf16[2048,1024]{1,0:T(8,128)(2,1)}) %all-gather.3.cloned.1.call-update) | async-done | bytes 4194320 | tf_op jit(solution)/shard_map/all_gather | solution.py:26
  46.2 4.8 fusion.58
  51.0 2.0 copy-done.6
  53.0 4.8 convolution_convert_fusion
  59.1 9.9 %all-to-all-start = ((s32[32,1,8]{2,1,0:T(1,128)}), s32[32,1,8]{2,1,0:T(1,128)S(1)}, u32[]{:S(2)}, u32[]{:S(2)}) async-start(s32[32,1,8]{2,1,0:T(1,128)} %bitcast.2), calls=%async_computation.1 | async-start | bytes 32768 | tf_op jit(solution)/shard_map/all_to_all | solution.py:42
  69.0 26.2 %reduce-scatter.6.cloned.1.call-done = bf16[256,1024]{1,0:T(8,128)(2,1)} async-done(((bf16[2048,1024]{1,0:T(8,128)(2,1)}), bf16[256,1024]{1,0:T(8,128)(2,1)}) %reduce-scatter.6.cloned.1.call-update) | async-done | bytes 524304 | tf_op jit(solution)/shard_map/reduce_scatter | solution.py:29
  96.4 2.2 fusion.54
  98.6 9.6 %all-to-all-start.2 = ((bf16[32,8,1024]{2,1,0:T(8,128)(2,1)}), bf16[32,8,1024]{2,1,0:T(8,128)(2,1)S(1)}, u32[]{:S(2)}, u32[]{:S(2)}) async-start(bf16[32,8,1024]{2,1,0:T(8,128)(2,1)} %get-tuple-element.19), calls=%async_computation.3 | async-start | bytes 1048576 | tf_op jit(solution)/shard_map/all_to_all | solution.py:39
  109.8 16.9 %all-to-all-done.2 = bf16[32,8,1024]{2,1,0:T(8,128)(2,1)S(1)} async-done(((bf16[32,8,1024]{2,1,0:T(8,128)(2,1)}), bf16[32,8,1024]{2,1,0:T(8,128)(2,1)S(1)}, u32[]{:S(2)}, u32[]{:S(2)}) %all-to-all-start.2) | async-done | bytes 524320 | tf_op jit(solution)/shard_map/all_to_all | solution.py:39
  126.8 4.7 all-to-all-start.1
  132.4 1.3 copy.46
  133.8 7.7 all-to-all-done.1
  141.5 4.0 all-to-all-start.3
  145.6 37.7 %all-to-all-done.3 = bf16[3,32,8,1024]{3,2,0,1:T(8,128)(2,1)S(1)} async-done(((bf16[3,32,8,1024]{3,2,0,1:T(8,128)(2,1)}), bf16[3,32,8,1024]{3,2,0,1:T(8,128)(2,1)S(1)}, u32[]{:S(2)}, u32[]{:S(2)}) %all-to-all-start.3) | async-done | bytes 1572896 | tf_op jit(solution)/shard_map/all_to_all | solution.py:50
  183.5 2.1 fusion.31
  187.2 75.9 %all_to_all.37 = f32[3,32,8,1024]{3,2,0,1:T(8,128)S(1)} all-to-all(f32[3,32,8,1024]{3,2,0,1:T(8,128)S(1)} %copy.50), channel_id=1, replica_groups=mesh['dp'=8,'group'=32] {'group'}, dimensions={1} | all-to-all | bytes 6291456 | tf_op jit(solution)/shard_map/all_to_all | solution.py:63
  263.2 3.1 fusion.14
  266.9 31.0 %all_to_all.38 = f32[32,8,1024]{2,1,0:T(8,128)S(1)} all-to-all(f32[32,8,1024]{2,1,0:T(8,128)S(1)} %copy.52), channel_id=1, replica_groups=mesh['dp'=8,'group'=32] {'group'}, dimensions={0} | all-to-all | bytes 2097152 | tf_op jit(solution)/shard_map/all_to_all | solution.py:74
  300.9 33.7 %all-gather.5.cloned.1.call-done = bf16[2048,1024]{1,0:T(8,128)(2,1)} async-done(((bf16[256,1024]{1,0:T(8,128)(2,1)}), bf16[2048,1024]{1,0:T(8,128)(2,1)}) %all-gather.5.cloned.1.call-update) | async-done | bytes 4194320 | tf_op jit(solution)/shard_map/all_gather | solution.py:77
  334.6 11.6 %fusion.11 = f32[1024,512]{0,1:T(8,128)S(1)} fusion(bf16[2048,1024]{1,0:T(8,128)(2,1)} %all-gather.3.cloned.1.call-done, f32[2048,512]{1,0:T(8,128)} %copy-done.6, bf16[2048,1024]{1,0:T(8,128)(2,1)} %all-gather.5.cloned.1.call-done, bf16[512,1024]{1,0:T(8,128)(2,1)S(1)} %copy-done), kind=kOutput, calls=%fused_computation.18 | convolution fusion | flops 4315938816 | bytes 15728640 | tf_op jit(solution)/shard_map/dot_general | solution.py:85
  346.2 1.9 copy.56
  348.1 7.3 fusion.55
  355.5 210.5 %reduce-scatter.10.cloned.1.call-done = f32[32,512]{1,0:T(8,128)} async-done(((f32[1024,512]{1,0:T(8,128)}), f32[32,512]{1,0:T(8,128)}) %reduce-scatter.10.cloned.1.call-update) | async-done | bytes 65552
  566.0 219.4 %reduce-scatter.8.cloned.1.call-done = f32[512,32]{0,1:T(8,128)} async-done(((f32[512,1024]{0,1:T(8,128)}), f32[512,32]{0,1:T(8,128)}) %reduce-scatter.8.cloned.1.call-update) | async-done | bytes 65552 | tf_op jit(solution)/shard_map/reduce_scatter | solution.py:90
  (47 shorter events, 11.5 us)
Async XLA Ops:
  7.2 45.8 %copy-start = (bf16[512,1024]{1,0:T(8,128)(2,1)S(1)}, bf16[512,1024]{1,0:T(8,128)(2,1)}, u32[]{:S(2)}) copy-start(bf16[512,1024]{1,0:T(8,128)(2,1)} %param.9) | copy-start | bytes 3145732
  7.2 39.0 %all-gather.3.cloned.1.call-start = ((), (), s32[]{:S(2)}) async-start(), calls=%async_computation.9 | async-start | bytes 4718592 | tf_op jit(solution)/shard_map/all_gather | solution.py:26
  7.9 87.3 %reduce-scatter.6.cloned.1.call-start = ((), (), s32[]{:S(2)}) async-start(), calls=%async_computation.10 | async-start | bytes 4718592 | tf_op jit(solution)/shard_map/reduce_scatter | solution.py:29
  51.0 2.0 copy-start.6
  57.8 0.7 copy-start.5
  57.8 50.5 %copy-start.4 = (s32[32,3]{0,1:T(4,128)S(1)}, s32[32,3]{0,1:T(4,128)}, u32[]{:S(2)}) copy-start(s32[32,3]{0,1:T(4,128)} %param.7) | copy-start | bytes 1156
  59.1 39.5 %all-to-all-start = ((s32[32,1,8]{2,1,0:T(1,128)}), s32[32,1,8]{2,1,0:T(1,128)S(1)}, u32[]{:S(2)}, u32[]{:S(2)}) async-start(s32[32,1,8]{2,1,0:T(1,128)} %bitcast.2), calls=%async_computation.1 | async-start | bytes 32768 | tf_op jit(solution)/shard_map/all_to_all | solution.py:42
  98.6 28.1 %all-to-all-start.2 = ((bf16[32,8,1024]{2,1,0:T(8,128)(2,1)}), bf16[32,8,1024]{2,1,0:T(8,128)(2,1)S(1)}, u32[]{:S(2)}, u32[]{:S(2)}) async-start(bf16[32,8,1024]{2,1,0:T(8,128)(2,1)} %get-tuple-element.19), calls=%async_computation.3 | async-start | bytes 1048576 | tf_op jit(solution)/shard_map/all_to_all | solution.py:39
  126.8 14.7 %all-to-all-start.1 = ((s32[3,32,8]{2,0,1:T(4,128)}), s32[3,32,8]{2,0,1:T(4,128)S(1)}, u32[]{:S(2)}, u32[]{:S(2)}) async-start(s32[3,32,8]{2,0,1:T(4,128)} %copy_select_fusion), calls=%async_computation.2 | async-start | bytes 131072 | tf_op jit(solution)/shard_map/all_to_all | solution.py:51
  132.4 51.0 %copy-start.1 = (bf16[256,1024]{1,0:T(8,128)(2,1)S(1)}, bf16[256,1024]{1,0:T(8,128)(2,1)}, u32[]{:S(2)}) copy-start(bf16[256,1024]{1,0:T(8,128)(2,1)} %reduce-scatter.6.cloned.1.call-done) | copy-start | bytes 1572868
  141.5 41.9 %all-to-all-start.3 = ((bf16[3,32,8,1024]{3,2,0,1:T(8,128)(2,1)}), bf16[3,32,8,1024]{3,2,0,1:T(8,128)(2,1)S(1)}, u32[]{:S(2)}, u32[]{:S(2)}) async-start(bf16[3,32,8,1024]{3,2,0,1:T(8,128)(2,1)} %copy.46), calls=%async_computation.4 | async-start | bytes 3145728 | tf_op jit(solution)/shard_map/all_to_all | solution.py:50
  145.5 189.2 %all-gather.5.cloned.1.call-start = ((), (), s32[]{:S(2)}) async-start(), calls=%async_computation.11 | async-start | bytes 4718592 | tf_op jit(solution)/shard_map/all_gather | solution.py:77
  263.2 34.7 %copy-start.3 = (bf16[1,256,1024]{2,1,0:T(8,128)(2,1)S(1)}, bf16[1,256,1024]{2,1,0:T(8,128)(2,1)}, u32[]{:S(2)}) copy-start(bf16[1,256,1024]{2,1,0:T(8,128)(2,1)} %get-tuple-element.18) | copy-start | bytes 1572868
  298.8 1.0 copy-start.2
  300.9 265.1 %reduce-scatter.10.cloned.1.call-start = ((), (), s32[]{:S(2)}) async-start(), calls=%async_computation.13 | async-start | bytes 2162688
  348.1 437.3 %reduce-scatter.8.cloned.1.call-start = ((), (), s32[]{:S(2)}) async-start(), calls=%async_computation.12 | async-start | bytes 2162688 | tf_op jit(solution)/shard_map/reduce_scatter | solution.py:90
Sparse Core Ops, SparseCore 0:
  9.9 36.2 all-gather.2
  57.9 37.2 reduce-scatter.5
  301.0 33.5 all-gather.4
  348.2 217.7 reduce-scatter.9
  570.7 214.6 reduce-scatter.7
where the time goes:
time: 793 us; the launch traced here: 792 us
  waiting for transfers between devices  591 us (75%)
  blocking collectives  107 us (13%)
  matrix products  35.4 us (4%)
  starting transfers between devices  28.3 us (4%)
  between operations  14 us (2%)
  local copies, waits for them, and re-layouts  10.6 us (1%)
    reduce_scatter x1, waiting for transfers between devices, per_device(): lax.psum_scatter(second_local, 'group', scatter_dimension=1, tiled=True)  219 us
    unnamed x6, waiting for transfers between devices  211 us
    all_to_all x1, blocking collectives, per_device(): lax.all_to_all(grad_cand[1:].reshape(listed, owners, piece, width), 'grou...  75.9 us
    all_gather x1, waiting for transfers between devices, per_device(): gathered = lax.all_gather(embeds, 'dp', axis=0, tiled=True)  38.2 us
    all_to_all x1, waiting for transfers between devices, per_device(): lax.all_to_all(outgoing, 'group', split_axis=1, concat_axis=1, tiled=True)  37.7 us
    all_gather x1, waiting for transfers between devices, per_device(): lax.all_gather(grad_proj.astype(jnp.bfloat16), 'dp', axis=0, tiled=True)  33.7 us
    all_to_all x1, blocking collectives, per_device(): lax.all_to_all(summed, 'group', split_axis=0, concat_axis=0, tiled=True)  31 us
    reduce_scatter x1, waiting for transfers between devices, per_device(): lax.psum_scatter(jnp.dot(hidden, w_second, preferred_element_type=jnp.flo...  26.2 us
  transfers between devices with their start and end apart: 9, of which 8 were waited for; matrix products, arithmetic and copies ran while one was open for 2% of the time, Pallas kernels for 0%

commit v1 on v0

--- a/solution.py
+++ b/solution.py
@@ -23,7 +23,24 @@
     piece = block // owners
     width = w_second.shape[1]
     listed = neighbors.shape[1]
-    gathered = lax.all_gather(embeds, "dp", axis=0, tiled=True)
+    size, here, width_2 = (lax.axis_size("dp"), lax.axis_index("dp"), embeds.shape[0])
+    forward = [(i, (i + 1) % size) for i in range(size)]
+    left = [(i, (i - 1) % size) for i in range(size)]
+    out = jnp.zeros((*embeds.shape[:0], size * width_2, *embeds.shape[0 + 1 :]), embeds.dtype)
+    out = lax.dynamic_update_slice_in_dim(out, embeds, here * width_2, axis=0)
+    from_left = from_right = embeds
+    middle = size // 2
+    for step in range(1, middle + 1):
+        from_left = lax.ppermute(from_left, "dp", forward)
+        out = lax.dynamic_update_slice_in_dim(
+            out, from_left, (here - step) % size * width_2, axis=0
+        )
+        if step < size - middle:
+            from_right = lax.ppermute(from_right, "dp", left)
+            out = lax.dynamic_update_slice_in_dim(
+                out, from_right, (here + step) % size * width_2, axis=0
+            )
+    gathered = out
     pre = jnp.dot(gathered, w_first, preferred_element_type=jnp.float32)
     hidden = gelu_fwd(pre).astype(jnp.bfloat16)
     proj = lax.psum_scatter(

time: 793 us -> 785 us (0.990)
  waiting for transfers between devices: 591 us -> 577 us
    reduce_scatter x0 -> x1, waiting for transfers between devices: none -> 219 us  [per_device(): lax.psum_scatter(first_local, 'group', scatter_dimension=0, tiled=True)]
    unnamed x6 -> x4, waiting for transfers between devices: 211 us -> 0.07 us
    all_gather x1 -> x0, waiting for transfers between devices: 38.2 us -> none  [per_device(): gathered = lax.all_gather(embeds, 'dp', axis=0, tiled=True)]
    ppermute x0 -> x7, waiting for transfers between devices: none -> 27.7 us  [the longest x4 27.7 us: per_device(): from_left = lax.ppermute(from_left, 'dp', forward)]
    reduce_scatter x1, waiting for transfers between devices: 219 us -> 205 us  [per_device(): lax.psum_scatter(second_local, 'group', scatter_dimension=1, tiled=True)]
  transfers between devices with their start and end apart: 9 -> 15, of which waited for: 8 -> 11; matrix products, arithmetic and copies ran while one was open for 2% -> 3% of each run, Pallas kernels for 0% -> 0%
where the time goes in v1:
time: 785 us; the launch traced here: 784 us
  waiting for transfers between devices  577 us (74%)
  blocking collectives  107 us (14%)
  starting transfers between devices  35.7 us (5%)
  matrix products  33.5 us (4%)
  between operations  14.1 us (2%)
  local copies, waits for them, and re-layouts  11.7 us (1%)
    reduce_scatter x1, waiting for transfers between devices, per_device(): lax.psum_scatter(first_local, 'group', scatter_dimension=0, tiled=True)  219 us
    reduce_scatter x1, waiting for transfers between devices, per_device(): lax.psum_scatter(second_local, 'group', scatter_dimension=1, tiled=True)  205 us
    all_to_all x1, blocking collectives, per_device(): lax.all_to_all(grad_cand[1:].reshape(listed, owners, piece, width), 'grou...  75.9 us
    all_to_all x1, waiting for transfers between devices, per_device(): lax.all_to_all(outgoing, 'group', split_axis=1, concat_axis=1, tiled=True)  37.7 us
    all_gather x1, waiting for transfers between devices, per_device(): lax.all_gather(grad_proj.astype(jnp.bfloat16), 'dp', axis=0, tiled=True)  33.6 us
    all_to_all x1, blocking collectives, per_device(): lax.all_to_all(summed, 'group', split_axis=0, concat_axis=0, tiled=True)  31 us
    reduce_scatter x1, waiting for transfers between devices, per_device(): lax.psum_scatter(jnp.dot(hidden, w_second, preferred_element_type=jnp.flo...  28.4 us
    ppermute x4, waiting for transfers between devices, per_device(): from_left = lax.ppermute(from_left, 'dp', forward)  27.7 us
  transfers between devices with their start and end apart: 15, of which 11 were waited for; matrix products, arithmetic and copies ran while one was open for 3% of the time, Pallas kernels for 0%

profile of v1, /device:TPU:4, one launch (start us, length us, event | category | flops | bytes accessed | tf_op | source)
XLA Modules:
  0.0 784.4 jit_solution(5708823436211058588)
XLA Ops:
  9.0 7.1 collective-permute-done
  17.8 7.0 collective-permute-done.2
  27.2 6.4 collective-permute-done.4
  34.9 7.3 collective-permute-done.6
  44.2 2.3 fusion.55
  48.6 4.7 convolution_convert_fusion
  54.7 11.5 %all-to-all-start = ((s32[32,1,8]{2,1,0:T(1,128)}), s32[32,1,8]{2,1,0:T(1,128)S(1)}, u32[]{:S(2)}, u32[]{:S(2)}) async-start(s32[32,1,8]{2,1,0:T(1,128)} %bitcast.2), calls=%async_computation.1 | async-start | bytes 32768 | tf_op jit(solution)/shard_map/all_to_all | solution.py:59
  66.2 28.4 %reduce-scatter.4.cloned.1.call-done = bf16[256,1024]{1,0:T(8,128)(2,1)} async-done(((bf16[2048,1024]{1,0:T(8,128)(2,1)}), bf16[256,1024]{1,0:T(8,128)(2,1)}) %reduce-scatter.4.cloned.1.call-update) | async-done | bytes 524304 | tf_op jit(solution)/shard_map/reduce_scatter | solution.py:46
  95.8 2.2 fusion.51
  98.0 9.7 %all-to-all-start.2 = ((bf16[32,8,1024]{2,1,0:T(8,128)(2,1)}), bf16[32,8,1024]{2,1,0:T(8,128)(2,1)S(1)}, u32[]{:S(2)}, u32[]{:S(2)}) async-start(bf16[32,8,1024]{2,1,0:T(8,128)(2,1)} %get-tuple-element.4), calls=%async_computation.3 | async-start | bytes 1048576 | tf_op jit(solution)/shard_map/all_to_all | solution.py:56
  109.3 16.8 %all-to-all-done.2 = bf16[32,8,1024]{2,1,0:T(8,128)(2,1)S(1)} async-done(((bf16[32,8,1024]{2,1,0:T(8,128)(2,1)}), bf16[32,8,1024]{2,1,0:T(8,128)(2,1)S(1)}, u32[]{:S(2)}, u32[]{:S(2)}) %all-to-all-start.2) | async-done | bytes 524320 | tf_op jit(solution)/shard_map/all_to_all | solution.py:56
  126.2 4.9 all-to-all-start.1
  133.3 7.7 all-to-all-done.1
  141.0 4.0 all-to-all-start.3
  145.2 37.7 %all-to-all-done.3 = bf16[3,32,8,1024]{3,2,0,1:T(8,128)(2,1)S(1)} async-done(((bf16[3,32,8,1024]{3,2,0,1:T(8,128)(2,1)}), bf16[3,32,8,1024]{3,2,0,1:T(8,128)(2,1)S(1)}, u32[]{:S(2)}, u32[]{:S(2)}) %all-to-all-start.3) | async-done | bytes 1572896 | tf_op jit(solution)/shard_map/all_to_all | solution.py:67
  183.0 2.1 fusion.28
  186.8 75.9 %all_to_all.37 = f32[3,32,8,1024]{3,2,0,1:T(8,128)S(1)} all-to-all(f32[3,32,8,1024]{3,2,0,1:T(8,128)S(1)} %copy.46), channel_id=1, replica_groups=mesh['dp'=8,'group'=32] {'group'}, dimensions={1} | all-to-all | bytes 6291456 | tf_op jit(solution)/shard_map/all_to_all | solution.py:80
  262.7 3.1 fusion.11
  266.4 31.0 %all_to_all.38 = f32[32,8,1024]{2,1,0:T(8,128)S(1)} all-to-all(f32[32,8,1024]{2,1,0:T(8,128)S(1)} %copy.48), channel_id=1, replica_groups=mesh['dp'=8,'group'=32] {'group'}, dimensions={0} | all-to-all | bytes 2097152 | tf_op jit(solution)/shard_map/all_to_all | solution.py:91
  299.6 33.6 %all-gather.2.cloned.1.call-done = bf16[2048,1024]{1,0:T(8,128)(2,1)} async-done(((bf16[256,1024]{1,0:T(8,128)(2,1)}), bf16[2048,1024]{1,0:T(8,128)(2,1)}) %all-gather.2.cloned.1.call-update) | async-done | bytes 4194320 | tf_op jit(solution)/shard_map/all_gather | solution.py:94
  333.3 7.3 fusion.52
  340.8 12.2 %fusion.9 = f32[1024,512]{1,0:T(8,128)} fusion(bf16[2048,1024]{1,0:T(8,128)(2,1)} %copy-done.2, f32[2048,512]{1,0:T(8,128)} %copy-done.11, bf16[2048,1024]{1,0:T(8,128)(2,1)} %all-gather.2.cloned.1.call-done, bf16[512,1024]{1,0:T(8,128)(2,1)S(1)} %copy-done), kind=kOutput, calls=%fused_computation.17 | convolution fusion | flops 4315938816 | bytes 15728640 | tf_op jit(solution)/shard_map/dot_general | solution.py:102
  353.1 205.4 %reduce-scatter.8.cloned.1.call-done = f32[512,32]{0,1:T(8,128)} async-done(((f32[512,1024]{0,1:T(8,128)}), f32[512,32]{0,1:T(8,128)}) %reduce-scatter.8.cloned.1.call-update) | async-done | bytes 65552 | tf_op jit(solution)/shard_map/reduce_scatter | solution.py:107
  558.5 219.4 %reduce-scatter.6.cloned.1.call-done = f32[32,512]{1,0:T(8,128)} async-done(((f32[1024,512]{1,0:T(8,128)}), f32[32,512]{1,0:T(8,128)}) %reduce-scatter.6.cloned.1.call-update) | async-done | bytes 65552 | tf_op jit(solution)/shard_map/reduce_scatter | solution.py:106
  (76 shorter events, 22.6 us)
Async XLA Ops:
  7.2 41.4 %copy-start = (bf16[512,1024]{1,0:T(8,128)(2,1)S(1)}, bf16[512,1024]{1,0:T(8,128)(2,1)}, u32[]{:S(2)}) copy-start(bf16[512,1024]{1,0:T(8,128)(2,1)} %param.9) | copy-start | bytes 3145732
  7.2 18.1 %copy-start.4 = (bf16[256,1024]{1,0:T(8,128)(2,1)S(1)}, bf16[256,1024]{1,0:T(8,128)(2,1)}, u32[]{:S(2)}) copy-start(bf16[256,1024]{1,0:T(8,128)(2,1)} %param.5) | copy-start | bytes 1572868
  7.2 87.4 %reduce-scatter.4.cloned.1.call-start = ((), (), s32[]{:S(2)}) async-start(), calls=%async_computation.9 | async-start | bytes 4718592 | tf_op jit(solution)/shard_map/reduce_scatter | solution.py:46
  7.2 8.8 %collective-permute-start = (bf16[256,1024]{1,0:T(8,128)(2,1)}, bf16[256,1024]{1,0:T(8,128)(2,1)S(1)}, u32[]{:S(2)}, u32[]{:S(2)}) collective-permute-start(bf16[256,1024]{1,0:T(8,128)(2,1)} %param.5), channel_id=1, source_target_pairs={{0,32},{32,64},{64,96},{96,128},{128,160},{160,192},{192,224},{224... | collective-permute-start | bytes 1572872 | tf_op jit(solution)/shard_map/ppermute | solution.py:34
  7.3 8.8 %collective-permute-start.1 = (bf16[256,1024]{1,0:T(8,128)(2,1)}, bf16[256,1024]{1,0:T(8,128)(2,1)S(1)}, u32[]{:S(2)}, u32[]{:S(2)}) collective-permute-start(bf16[256,1024]{1,0:T(8,128)(2,1)} %param.5), channel_id=1, source_target_pairs={{0,224},{32,0},{64,32},{96,64},{128,96},{160,128},{192,160},{224,1... | collective-permute-start | bytes 1572872 | tf_op jit(solution)/shard_map/ppermute | solution.py:39
  16.1 8.7 %collective-permute-start.2 = (bf16[256,1024]{1,0:T(8,128)(2,1)S(1)}, bf16[256,1024]{1,0:T(8,128)(2,1)}, u32[]{:S(2)}, u32[]{:S(2)}) collective-permute-start(bf16[256,1024]{1,0:T(8,128)(2,1)S(1)} %collective-permute-done), channel_id=1, source_target_pairs={{0,32},{32,64},{64,96},{96,128},{128,160},{160,192},{192,224},{224... | collective-permute-start | bytes 1572872 | tf_op jit(solution)/shard_map/ppermute | solution.py:34
  16.1 9.3 %collective-permute-start.3 = (bf16[256,1024]{1,0:T(8,128)(2,1)S(1)}, bf16[256,1024]{1,0:T(8,128)(2,1)S(1)}, u32[]{:S(2)}, u32[]{:S(2)}) collective-permute-start(bf16[256,1024]{1,0:T(8,128)(2,1)S(1)} %collective-permute-done.1), channel_id=1, source_target_pairs={{0,224},{32,0},{64,32},{96,64},{128,96},{160,128},{192,160},{224,1... | collective-permute-start | bytes 1572872 | tf_op jit(solution)/shard_map/ppermute | solution.py:39
  24.8 8.8 %collective-permute-start.4 = (bf16[256,1024]{1,0:T(8,128)(2,1)}, bf16[256,1024]{1,0:T(8,128)(2,1)S(1)}, u32[]{:S(2)}, u32[]{:S(2)}) collective-permute-start(bf16[256,1024]{1,0:T(8,128)(2,1)} %collective-permute-done.2), channel_id=1, source_target_pairs={{0,32},{32,64},{64,96},{96,128},{128,160},{160,192},{192,224},{224... | collective-permute-start | bytes 1572872 | tf_op jit(solution)/shard_map/ppermute | solution.py:34
  24.8 2.4 copy-start.6
  25.3 18.9 %copy-start.10 = (bf16[1024,512]{1,0:T(8,128)(2,1)S(1)}, bf16[1024,512]{1,0:T(8,128)(2,1)}, u32[]{:S(2)}) copy-start(bf16[1024,512]{1,0:T(8,128)(2,1)} %param.8) | copy-start | bytes 3145732
  25.4 9.4 %collective-permute-start.5 = (bf16[256,1024]{1,0:T(8,128)(2,1)S(1)}, bf16[256,1024]{1,0:T(8,128)(2,1)S(1)}, u32[]{:S(2)}, u32[]{:S(2)}) collective-permute-start(bf16[256,1024]{1,0:T(8,128)(2,1)S(1)} %collective-permute-done.3), channel_id=1, source_target_pairs={{0,224},{32,0},{64,32},{96,64},{128,96},{160,128},{192,160},{224,1... | collective-permute-start | bytes 1572872 | tf_op jit(solution)/shard_map/ppermute | solution.py:39
  33.6 8.6 %collective-permute-start.6 = (bf16[256,1024]{1,0:T(8,128)(2,1)S(1)}, bf16[256,1024]{1,0:T(8,128)(2,1)S(1)}, u32[]{:S(2)}, u32[]{:S(2)}) collective-permute-start(bf16[256,1024]{1,0:T(8,128)(2,1)S(1)} %collective-permute-done.4), channel_id=1, source_target_pairs={{0,32},{32,64},{64,96},{96,128},{128,160},{160,192},{192,224},{224... | collective-permute-start | bytes 1572872 | tf_op jit(solution)/shard_map/ppermute | solution.py:34
  46.5 2.0 copy-start.11
  53.3 54.5 %copy-start.8 = (s32[32,3]{0,1:T(4,128)S(1)}, s32[32,3]{0,1:T(4,128)}, u32[]{:S(2)}) copy-start(s32[32,3]{0,1:T(4,128)} %param.7) | copy-start | bytes 1156
  54.7 43.3 %all-to-all-start = ((s32[32,1,8]{2,1,0:T(1,128)}), s32[32,1,8]{2,1,0:T(1,128)S(1)}, u32[]{:S(2)}, u32[]{:S(2)}) async-start(s32[32,1,8]{2,1,0:T(1,128)} %bitcast.2), calls=%async_computation.1 | async-start | bytes 32768 | tf_op jit(solution)/shard_map/all_to_all | solution.py:59
  98.0 28.2 %all-to-all-start.2 = ((bf16[32,8,1024]{2,1,0:T(8,128)(2,1)}), bf16[32,8,1024]{2,1,0:T(8,128)(2,1)S(1)}, u32[]{:S(2)}, u32[]{:S(2)}) async-start(bf16[32,8,1024]{2,1,0:T(8,128)(2,1)} %get-tuple-element.4), calls=%async_computation.3 | async-start | bytes 1048576 | tf_op jit(solution)/shard_map/all_to_all | solution.py:56
  126.2 14.9 %all-to-all-start.1 = ((s32[3,32,8]{2,0,1:T(4,128)}), s32[3,32,8]{2,0,1:T(4,128)S(1)}, u32[]{:S(2)}, u32[]{:S(2)}) async-start(s32[3,32,8]{2,0,1:T(4,128)} %copy_select_fusion), calls=%async_computation.2 | async-start | bytes 131072 | tf_op jit(solution)/shard_map/all_to_all | solution.py:68
  132.0 51.0 %copy-start.1 = (bf16[256,1024]{1,0:T(8,128)(2,1)S(1)}, bf16[256,1024]{1,0:T(8,128)(2,1)}, u32[]{:S(2)}) copy-start(bf16[256,1024]{1,0:T(8,128)(2,1)} %reduce-scatter.4.cloned.1.call-done) | copy-start | bytes 1572868
  141.0 41.9 %all-to-all-start.3 = ((bf16[3,32,8,1024]{3,2,0,1:T(8,128)(2,1)}), bf16[3,32,8,1024]{3,2,0,1:T(8,128)(2,1)S(1)}, u32[]{:S(2)}, u32[]{:S(2)}) async-start(bf16[3,32,8,1024]{3,2,0,1:T(8,128)(2,1)} %copy.42), calls=%async_computation.4 | async-start | bytes 3145728 | tf_op jit(solution)/shard_map/all_to_all | solution.py:67
  145.0 188.3 %all-gather.2.cloned.1.call-start = ((), (), s32[]{:S(2)}) async-start(), calls=%async_computation.10 | async-start | bytes 4718592 | tf_op jit(solution)/shard_map/all_gather | solution.py:94
  262.7 34.7 %copy-start.7 = (bf16[1,256,1024]{2,1,0:T(8,128)(2,1)S(1)}, bf16[1,256,1024]{2,1,0:T(8,128)(2,1)}, u32[]{:S(2)}) copy-start(bf16[1,256,1024]{2,1,0:T(8,128)(2,1)} %get-tuple-element.3) | copy-start | bytes 1572868
  298.4 42.2 %copy-start.3 = (f32[256,1024]{1,0:T(8,128)}, f32[256,1024]{1,0:T(8,128)S(1)}, u32[]{:S(2)}) copy-start(f32[256,1024]{1,0:T(8,128)S(1)} %get-tuple-element.6) | copy-start | bytes 3145732
  299.6 258.9 %reduce-scatter.8.cloned.1.call-start = ((), (), s32[]{:S(2)}) async-start(), calls=%async_computation.12 | async-start | bytes 2162688 | tf_op jit(solution)/shard_map/reduce_scatter | solution.py:107
  340.6 437.3 %reduce-scatter.6.cloned.1.call-start = ((), (), s32[]{:S(2)}) async-start(), calls=%async_computation.11 | async-start | bytes 2162688 | tf_op jit(solution)/shard_map/reduce_scatter | solution.py:106
  (3 other events, 4.4 us)
Sparse Core Ops, SparseCore 0:
  53.5 41.0 reduce-scatter.3
  299.7 33.5 all-gather.1
  340.7 217.7 reduce-scatter.7
  563.2 214.6 reduce-scatter.5
